TPU v7x, 32 devices: a whole 2x2x4 slice. The times are simulated.
32 devices in a mesh: row: 8 (over y, x, core), col: 4 (over z).
Axes of the slice: x: 2, y: 2, z: 4, core: 2. Of those that a mesh axis runs over, the one named last changes fastest.
Arguments:
- vectors: bfloat16 [4, 16384], P(None, ('row', 'col')), may hold values from -6 to 6
- tile_values: bfloat16 [8, 4, 32, 4096], P('row', 'col'), may hold values from -0.75 to 0.75
- tile_rows: int32 [8, 4, 32], P('row', 'col'), may hold values from 0 to 31, as said below
- tile_cols: int32 [8, 4, 32], P('row', 'col'), may hold values from 0 to 63
- tile_scale: int32 [8, 4, 32], P('row', 'col'), may hold values from 0 to 63
- tile_count: int32 [8, 4], P('row', 'col'), may hold values from 2 to 32, as said below
- scale_table: float32 [64], replicated, may hold values from 0.1 to 1.5
Outputs:
- product: float32 [4, 16384], P(None, ('row', 'col'))
Inputs may be any that keep to these rules, and one draw needn't show every extreme that they name: Slots 0 to tile_count - 1 of a device hold its tiles, later slots are ignored; some device has all 32 slots live. On device (r, c), each slot t below min(8, 2) holds a diagonal block: tile_rows[r, c, t] = c * 8 + t; the other slots are uniform over the range.
All inputs are finite; a program needn't handle non-finite values.
Results may differ from a plain program's by a relative error of at most 0.0003.
Values may be sent and summed in bfloat16 or wider, within the bound.
A program may use at most 64 MiB of HBM per device.

v0:
```python
import jax
import jax.numpy as jnp
from jax import lax
from jax.sharding import PartitionSpec as P

TILE = 64
NVEC = 4


def block_weights(
    row_ids,
    col_ids,
    scale_ids,
    live_count,
    scale_table,
    row_index,
    col_index,
    piece_blocks,
    col_total,
):
    global_row = row_index * col_total * piece_blocks + row_ids
    global_col = (
        col_ids // piece_blocks * col_total + col_index
    ) * piece_blocks + col_ids % piece_blocks
    table_hit = scale_ids[:, None] == jnp.arange(scale_table.shape[0], dtype=jnp.int32)[None, :]
    looked = jnp.sum(jnp.where(table_hit, scale_table[None, :], 0.0), axis=1)
    halved = jnp.where(global_row == global_col, 0.5, 1.0) * looked
    is_live = jnp.arange(row_ids.shape[0], dtype=jnp.int32) < live_count
    return jnp.where(is_live, halved, 0.0)


def tile_sums(row_vec, col_vec, values, row_ids, col_ids, weight_of, row_start, col_start):
    matrices = values.reshape(-1, TILE, TILE)
    near = jnp.take(row_vec, row_ids, axis=1)
    distant = jnp.take(col_vec, col_ids, axis=1)
    forward = (
        jnp.einsum("tij,ktj->kti", matrices, distant, preferred_element_type=jnp.float32)
        * weight_of[None, :, None]
    )
    mirrored = (
        jnp.einsum("tij,kti->ktj", matrices, near, preferred_element_type=jnp.float32)
        * weight_of[None, :, None]
    )
    return (row_start.at[:, row_ids].add(forward), col_start.at[:, col_ids].add(mirrored))


def per_device(vectors, tile_values, tile_rows, tile_cols, tile_scale, tile_count, scale_table):
    row_total = lax.axis_size("row")
    col_total = lax.axis_size("col")
    row_index = lax.axis_index("row")
    col_index = lax.axis_index("col")
    piece_len = vectors.shape[1]
    piece_blocks = piece_len // TILE
    row_blocks = col_total * piece_blocks
    col_blocks = row_total * piece_blocks
    row_vec = lax.all_gather(vectors, "col", axis=1, tiled=True).reshape(NVEC, row_blocks, TILE)
    col_vec = lax.all_gather(vectors, "row", axis=1, tiled=True).reshape(NVEC, col_blocks, TILE)
    row_ids = tile_rows.reshape(-1)
    col_ids = tile_cols.reshape(-1)
    scale_ids = tile_scale.reshape(-1)
    slot_total = row_ids.shape[0]
    values = tile_values.reshape(slot_total, TILE * TILE)
    live_count = tile_count.reshape(())
    weight_of = block_weights(
        row_ids,
        col_ids,
        scale_ids,
        live_count,
        scale_table,
        row_index,
        col_index,
        piece_blocks,
        col_total,
    )
    row_start = jnp.zeros((NVEC, row_blocks, TILE), jnp.float32)
    col_start = jnp.zeros((NVEC, col_blocks, TILE), jnp.float32)
    row_part, col_part = tile_sums(
        row_vec, col_vec, values, row_ids, col_ids, weight_of, row_start, col_start
    )
    row_flat = row_part.reshape(NVEC, row_blocks * TILE)
    col_flat = col_part.reshape(NVEC, col_blocks * TILE)
    own_row = lax.psum_scatter(row_flat, "col", scatter_dimension=1, tiled=True)
    received = lax.all_to_all(
        col_flat.reshape(NVEC, row_total, piece_len), "row", split_axis=1, concat_axis=0, tiled=True
    )
    own_col = jnp.sum(received.reshape(row_total, NVEC, piece_len), axis=0)
    return own_row + own_col


def solution(mesh):
    return jax.shard_map(
        per_device,
        mesh=mesh,
        in_specs=(
            P(None, ("row", "col")),
            P("row", "col", None, None),
            P("row", "col", None),
            P("row", "col", None),
            P("row", "col", None),
            P("row", "col"),
            P(),
        ),
        out_specs=P(None, ("row", "col")),
        check_vma=False,
    )
```

profile of v0, /device:TPU:0, one launch (start us, length us, event | category | flops | bytes accessed | tf_op | source)
XLA Modules:
  0.0 61.9 jit_solution(3947918317790185855)
XLA Ops:
  6.5 0.0 reduce-scatter.4.cloned.1.call-start
  6.5 0.6 %copy-done.2 = s32[1,1,32]{2,1,0:T(1,128)S(1)} copy-done((s32[1,1,32]{2,1,0:T(1,128)S(1)}, s32[1,1,32]{2,1,0:T(1,128)}, u32[]{:S(2)}) %copy-start.2) | copy-done | bytes 152
  7.9 0.7 %fusion.9 = s32[32]{0:T(128)S(1)} fusion(s32[1,1,32]{2,1,0:T(1,128)} %param.9), kind=kLoop, calls=%fused_computation.32 | loop fusion | flops 96 | bytes 256 | tf_op jit(solution)/shard_map/select_n | solution.py:44
  8.5 10.7 %all_gather.6 = bf16[4,4096]{1,0:T(4,128)(2,1)S(1)} all-gather(bf16[4,512]{1,0:T(4,128)(2,1)} %param.7), channel_id=1, replica_groups=mesh['row'=8,'col'=4] {'row'}, dimensions={1}, use_global_device_ids=true | all-gather | bytes 36864 | tf_op jit(solution)/shard_map/all_gather | solution.py:57
  19.2 0.1 reshape.163
  19.4 0.1 copy.19
  19.4 0.0 copy-done
  19.4 0.5 reshape_reshape.6
  20.0 0.0 copy-start.4
  20.0 0.0 copy-start.5
  20.0 0.6 %copy-done.4 = f32[64]{0:T(128)S(1)} copy-done((f32[64]{0:T(128)S(1)}, f32[64]{0:T(128)}, u32[]{:S(2)}) %copy-start.4) | copy-done | bytes 280
  20.6 0.0 copy-done.5
  20.7 0.2 select_reduce_fusion
  20.8 0.6 gather_fusion
  21.5 0.0 copy-start.3
  21.5 0.6 %copy-done.3 = s32[1,1,32]{2,1,0:T(1,128)S(1)} copy-done((s32[1,1,32]{2,1,0:T(1,128)S(1)}, s32[1,1,32]{2,1,0:T(1,128)}, u32[]{:S(2)}) %copy-start.3) | copy-done | bytes 152
  22.1 0.4 convolution_multiply_fusion.1
  22.6 1.7 %scatter_fusion = f32[4,32,64]{2,0,1:T(4,128)S(1)} fusion(f32[4,32,64]{2,0,1:T(4,128)S(1)} %broadcast_in_dim.54, s32[32]{0:T(128)S(1)} %fusion.9, f32[32,4,64]{2,1,0:T(4,128)S(1)} %convolution_multiply_fusion.1), kind=kCustom, calls=%fused_computation.2 | custom fusion | flops 8192 | bytes 98432 | tf_op jit(solution)/shard_map/scatter-add | solution.py:44
  24.2 1.4 %copy.26 = f32[4,32,64]{0,2,1:T(8,128)} copy(f32[4,32,64]{2,0,1:T(4,128)S(1)} %scatter_fusion) | data formatting | bytes 65536
  25.6 0.0 reduce-scatter.4.cloned.1.call-update
  25.7 0.0 copy-start.1
  25.7 0.7 %copy-done.1 = bf16[4,512]{1,0:T(4,128)(2,1)S(1)} copy-done((bf16[4,512]{1,0:T(4,128)(2,1)S(1)}, bf16[4,512]{1,0:T(4,128)(2,1)}, u32[]{:S(2)}) %copy-start.1) | copy-done | bytes 4120
  26.4 13.6 %all_gather.7 = bf16[4,2048]{1,0:T(4,128)(2,1)S(1)} all-gather(bf16[4,512]{1,0:T(4,128)(2,1)S(1)} %copy-done.1), channel_id=1, replica_groups=mesh['row'=8,'col'=4] {'col'}, dimensions={1}, use_global_device_ids=true | all-gather | bytes 20480 | tf_op jit(solution)/shard_map/all_gather | solution.py:56
  40.0 0.1 reshape.168
  40.1 0.6 gather_fusion.1
  40.7 0.3 convolution_multiply_fusion
  41.0 1.6 %scatter_fusion.1 = f32[4,64,64]{2,0,1:T(4,128)S(1)} fusion(f32[4,64,64]{2,0,1:T(4,128)S(1)} %broadcast_in_dim.62, s32[32]{0:T(128)S(1)} %fusion.10, f32[32,4,64]{2,1,0:T(4,128)S(1)} %convolution_multiply_fusion), kind=kCustom, calls=%fused_computation.3 | custom fusion | flops 8192 | bytes 98432 | tf_op jit(solution)/shard_map/scatter-add | solution.py:44
  42.7 0.1 reshape_reshape.7
  42.9 7.5 %all_to_all.4 = f32[4,8,512]{2,0,1:T(4,128)S(1)} all-to-all(f32[4,8,512]{2,0,1:T(4,128)S(1)} %copy.23), channel_id=1, replica_groups=mesh['row'=8,'col'=4] {'row'}, dimensions={1} | all-to-all | bytes 131072 | tf_op jit(solution)/shard_map/all_to_all | solution.py:83
  50.4 3.0 %reduce-scatter.4.cloned.1.call-done = f32[512,4]{1,0:T(8,128)} async-done(((f32[2048,4]{1,0:T(8,128)}), f32[512,4]{1,0:T(8,128)}) %reduce-scatter.4.cloned.1.call-update) | async-done | bytes 8208
  53.4 1.1 %copy.25 = f32[4,512]{1,0:T(4,128)S(1)} copy(f32[4,512]{0,1:T(8,128)} %bitcast.47) | data formatting | bytes 16384
  54.4 0.6 add.111
  (14 shorter events, 0.2 us)
Async XLA Ops:
  6.5 0.7 %copy-start.2 = (s32[1,1,32]{2,1,0:T(1,128)S(1)}, s32[1,1,32]{2,1,0:T(1,128)}, u32[]{:S(2)}) copy-start(s32[1,1,32]{2,1,0:T(1,128)} %param.10) | copy-start | bytes 388
  6.5 12.9 %copy-start = (bf16[1,1,32,4096]{3,2,1,0:T(8,128)(2,1)S(1)}, bf16[1,1,32,4096]{3,2,1,0:T(8,128)(2,1)}, u32[]{:S(2)}) copy-start(bf16[1,1,32,4096]{3,2,1,0:T(8,128)(2,1)} %param.8) | copy-start | bytes 786436
  6.5 46.8 %reduce-scatter.4.cloned.1.call-start = ((), (), s32[]{:S(2)}) async-start(), calls=%async_computation.2 | async-start | bytes 1310720
  20.0 0.7 %copy-start.4 = (f32[64]{0:T(128)S(1)}, f32[64]{0:T(128)}, u32[]{:S(2)}) copy-start(f32[64]{0:T(128)} %param.13) | copy-start | bytes 772
  20.0 0.7 %copy-start.5 = (s32[1,1,32]{2,1,0:T(1,128)S(1)}, s32[1,1,32]{2,1,0:T(1,128)}, u32[]{:S(2)}) copy-start(s32[1,1,32]{2,1,0:T(1,128)} %param.11) | copy-start | bytes 388
  21.5 0.7 %copy-start.3 = (s32[1,1,32]{2,1,0:T(1,128)S(1)}, s32[1,1,32]{2,1,0:T(1,128)}, u32[]{:S(2)}) copy-start(s32[1,1,32]{2,1,0:T(1,128)} %param.9) | copy-start | bytes 388
  25.7 0.7 %copy-start.1 = (bf16[4,512]{1,0:T(4,128)(2,1)S(1)}, bf16[4,512]{1,0:T(4,128)(2,1)}, u32[]{:S(2)}) copy-start(bf16[4,512]{1,0:T(4,128)(2,1)} %param.7) | copy-start | bytes 12292
Sparse Core Ops, SparseCore 0:
  25.8 27.5 reduce-scatter.3
where the time goes:
time: 62.2 us; the launch traced here: 61.9 us
  blocking collectives  31.9 us (51%)
  between operations  14.2 us (23%)
  local copies, waits for them, and re-layouts  7.3 us (12%)
  other arithmetic  4.82 us (8%)
  waiting for transfers between devices  3.01 us (5%)
  matrix products  0.74 us (1%)
    all_gather x1, blocking collectives, per_device(): lax.all_gather(vectors, 'col', axis=1, tiled=True)  13.6 us
    all_gather x1, blocking collectives, per_device(): lax.all_gather(vectors, 'row', axis=1, tiled=True)  10.7 us
    all_to_all x1, blocking collectives, per_device(): lax.all_to_all(col_flat.reshape(NVEC, row_total, piece_len), 'row', split...  7.51 us
    unnamed x14, local copies, waits for them, and re-layouts  5.06 us
    unnamed x2, waiting for transfers between devices  3.01 us
    scatter-add x1, other arithmetic, tile_sums(): row_start.at[:, row_ids].add(forward)  1.65 us
    scatter-add x1, other arithmetic, tile_sums(): col_start.at[:, col_ids].add(mirrored)  1.64 us
  transfers between devices with their start and end apart: 1, of which 1 were waited for; matrix products, arithmetic and copies ran while one was open for 5% of the time, Pallas kernels for 0%

commit v1 on v0

v1 whole, which is shorter than its diff:
```python
import functools

import jax
import jax.numpy as jnp
from jax import lax
from jax.experimental import pallas as pl
from jax.experimental.pallas import tpu as pltpu
from jax.sharding import PartitionSpec as P

TILE = 64
NVEC = 4
LANES = 128
GROUP = 4
MESH = pl.DeviceIdType.MESH


def kernel(
    n_row, n_col, slots, piece_len,
    x_hbm, w_hbm, rows_hbm, cols_hbm, scale_hbm, count_hbm, table_hbm,
    out_ref,
    col_x, row_x, w_vm, rows_sm, cols_sm, scale_sm, count_sm, table_sm,
    rid_vm, cid_vm, wt_vm, row_send, row_recv, col_send, col_recv,
    local_sem, x_row_send, x_row_recv, x_col_send, x_col_recv,
    p_row_send, p_row_recv, p_col_send, p_col_recv,
):
    me_row = lax.axis_index("row")
    me_col = lax.axis_index("col")
    blocks = piece_len // TILE
    chunk = piece_len * NVEC // LANES
    depth = slots * NVEC

    copies = [
        pltpu.make_async_copy(src, dst, local_sem.at[i])
        for i, (src, dst) in enumerate((
            (x_hbm, col_x.at[0]),
            (x_hbm, row_x.at[0]),
            (rows_hbm, rows_sm),
            (cols_hbm, cols_sm),
            (scale_hbm, scale_sm),
            (count_hbm, count_sm),
            (table_hbm, table_sm),
            (w_hbm, w_vm),
        ))
    ]
    for copy in copies:
        copy.start()

    def along_col(d):
        return (me_row, lax.rem(me_col + d, n_col))

    def along_row(d):
        return (lax.rem(me_row + d, n_row), me_col)

    barrier = pltpu.get_barrier_semaphore()
    for d in range(1, n_col):
        pl.semaphore_signal(barrier, inc=1, device_id=along_col(d), device_id_type=MESH)
    for d in range(1, n_row):
        pl.semaphore_signal(barrier, inc=1, device_id=along_row(d), device_id_type=MESH)
    copies[0].wait()
    copies[1].wait()
    pl.semaphore_wait(barrier, n_col + n_row - 2)

    gather_row = [
        pltpu.make_async_remote_copy(
            src_ref=row_x.at[0], dst_ref=row_x.at[d], send_sem=x_row_send.at[d],
            recv_sem=x_row_recv.at[d], device_id=along_col(d), device_id_type=MESH)
        for d in range(1, n_col)
    ]
    gather_col = [
        pltpu.make_async_remote_copy(
            src_ref=col_x.at[0], dst_ref=col_x.at[d], send_sem=x_col_send.at[d],
            recv_sem=x_col_recv.at[d], device_id=along_row(d), device_id_type=MESH)
        for d in range(1, n_row)
    ]
    for copy in gather_row + gather_col:
        copy.start()

    for copy in copies[2:7]:
        copy.wait()
    upper = lax.broadcasted_iota(jnp.int32, (8, LANES), 0) < NVEC
    for v in range(slots // 2):
        a, b = 2 * v, 2 * v + 1
        here = pl.ds(8 * v, 8)
        rid_vm[here, :] = jnp.where(upper, rows_sm[0, 0, a], rows_sm[0, 0, b])
        cid_vm[here, :] = jnp.where(upper, cols_sm[0, 0, a], cols_sm[0, 0, b])
        wt_vm[here, :] = jnp.where(
            upper, table_sm[scale_sm[0, 0, a]], table_sm[scale_sm[0, 0, b]])
    rid = rid_vm[...]
    cid = cid_vm[...]
    sub = lax.broadcasted_iota(jnp.int32, (depth, LANES), 0)
    lane = lax.broadcasted_iota(jnp.int32, (depth, LANES), 1)
    half = lax.div(lane, TILE)
    rid_piece, rid_block = lax.div(rid, blocks), lax.rem(rid, blocks)
    cid_piece, cid_block = lax.div(cid, blocks), lax.rem(cid, blocks)
    global_row = me_row * (n_col * blocks) + rid
    global_col = (cid_piece * n_col + me_col) * blocks + cid_block
    weight = jnp.where(global_row == global_col, 0.5, 1.0) * wt_vm[...]
    weight = jnp.where(lax.div(sub, NVEC) < count_sm[0, 0], weight, 0.0)

    def places(piece, block, me, total):
        back = lax.rem(me - piece + total, total)
        target = back * chunk + lax.div(block, 2) * NVEC + lax.rem(sub, NVEC)
        across = lax.broadcasted_iota(jnp.int32, (depth, total * chunk), 1)
        down = lax.broadcasted_iota(jnp.int32, (total * chunk, depth), 0)
        take = jnp.where(across == target[:, :1], 1.0, 0.0).astype(jnp.bfloat16)
        put = jnp.where(down == jnp.transpose(target)[:1, :], 1.0, 0.0).astype(jnp.bfloat16)
        return take, jnp.concatenate([put, put], axis=1), lax.rem(block, 2)

    take_row, put_row, odd_row = places(rid_piece, rid_block, me_col, n_col)
    take_col, put_col, odd_col = places(cid_piece, cid_block, me_row, n_row)
    row_weight = jnp.where(half == odd_row, weight, 0.0)
    col_weight = jnp.where(half == odd_col, weight, 0.0)

    def pick(take, pieces, odd):
        both = jnp.dot(take, pieces, preferred_element_type=jnp.float32)
        kept = jnp.where(half == odd, both, 0.0)
        return (kept + pltpu.roll(kept, TILE, 1)).astype(jnp.bfloat16)

    def place(put, values):
        high = values.astype(jnp.bfloat16)
        low = (values - high.astype(jnp.float32)).astype(jnp.bfloat16)
        return jnp.dot(
            put, jnp.concatenate([high, low], axis=0), preferred_element_type=jnp.float32)

    rows_of = GROUP * NVEC
    wide = GROUP * TILE
    g_row = lax.div(lax.broadcasted_iota(jnp.int32, (rows_of, wide), 0), NVEC)
    g_col = lax.div(lax.broadcasted_iota(jnp.int32, (rows_of, wide), 1), TILE)
    same = g_row == g_col
    copies[7].wait()

    for copy in gather_col:
        copy.wait_recv()
    distant = pick(take_col, col_x[...].reshape(n_row * chunk, LANES), odd_col)
    parts = []
    for g in range(slots // GROUP):
        tiles = w_vm[g * wide:(g + 1) * wide, :]
        prod = lax.dot_general(
            distant[g * rows_of:(g + 1) * rows_of, :TILE], tiles, (((1,), (1,)), ((), ())),
            preferred_element_type=jnp.float32)
        prod = jnp.where(same, prod, 0.0)
        total = prod[:, :LANES]
        for i in range(LANES, wide, LANES):
            total = total + prod[:, i:i + LANES]
        parts.append(total + pltpu.roll(total, TILE, 1))
    forward = jnp.concatenate(parts, axis=0) * row_weight
    row_send[...] = place(put_row, forward).reshape(n_col, chunk, LANES)
    scatter_row = [
        pltpu.make_async_remote_copy(
            src_ref=row_send.at[d], dst_ref=row_recv.at[d], send_sem=p_row_send.at[d],
            recv_sem=p_row_recv.at[d], device_id=along_col(n_col - d), device_id_type=MESH)
        for d in range(1, n_col)
    ]
    for copy in scatter_row:
        copy.start()

    for copy in gather_row:
        copy.wait_recv()
    near = pick(take_row, row_x[...].reshape(n_col * chunk, LANES), odd_row)
    parts = []
    for g in range(slots // GROUP):
        tiles = w_vm[g * wide:(g + 1) * wide, :]
        left = near[g * rows_of:(g + 1) * rows_of, :]
        left = jnp.concatenate([left] * (wide // LANES), axis=1)
        left = jnp.where(same, left, jnp.zeros_like(left))
        prod = jnp.dot(left, tiles, preferred_element_type=jnp.float32)
        parts.append(jnp.concatenate([prod, prod], axis=1))
    mirrored = jnp.concatenate(parts, axis=0) * col_weight
    col_send[...] = place(put_col, mirrored).reshape(n_row, chunk, LANES)
    scatter_col = [
        pltpu.make_async_remote_copy(
            src_ref=col_send.at[d], dst_ref=col_recv.at[d], send_sem=p_col_send.at[d],
            recv_sem=p_col_recv.at[d], device_id=along_row(n_row - d), device_id_type=MESH)
        for d in range(1, n_row)
    ]
    for copy in scatter_col:
        copy.start()

    total = row_send[0] + col_send[0]
    for copy in gather_row + gather_col:
        copy.wait_send()
    for d, copy in enumerate(scatter_row, 1):
        copy.wait_recv()
        total = total + row_recv[d]
    for d, copy in enumerate(scatter_col, 1):
        copy.wait_recv()
        total = total + col_recv[d]
    out_ref[...] = total
    for copy in scatter_row + scatter_col:
        copy.wait_send()


def per_device(vectors, tile_values, tile_rows, tile_cols, tile_scale, tile_count, scale_table):
    n_row = lax.axis_size("row")
    n_col = lax.axis_size("col")
    piece_len = vectors.shape[1]
    slots = tile_rows.shape[-1]
    groups = piece_len // LANES
    chunk = groups * NVEC
    depth = slots * NVEC
    x = vectors.reshape(NVEC, groups, LANES).transpose(1, 0, 2).reshape(chunk, LANES)
    w = tile_values.reshape(slots * TILE, TILE)
    dma = pltpu.SemaphoreType.DMA
    out = pl.pallas_call(
        functools.partial(kernel, n_row, n_col, slots, piece_len),
        out_shape=jax.ShapeDtypeStruct((chunk, LANES), jnp.float32),
        in_specs=[pl.BlockSpec(memory_space=pl.ANY)] * 7,
        out_specs=pl.BlockSpec(memory_space=pltpu.VMEM),
        scratch_shapes=[
            pltpu.VMEM((n_row, chunk, LANES), jnp.bfloat16),
            pltpu.VMEM((n_col, chunk, LANES), jnp.bfloat16),
            pltpu.VMEM((slots * TILE, TILE), jnp.bfloat16),
            pltpu.SMEM(tile_rows.shape, jnp.int32),
            pltpu.SMEM(tile_cols.shape, jnp.int32),
            pltpu.SMEM(tile_scale.shape, jnp.int32),
            pltpu.SMEM(tile_count.shape, jnp.int32),
            pltpu.SMEM(scale_table.shape, jnp.float32),
            pltpu.VMEM((depth, LANES), jnp.int32),
            pltpu.VMEM((depth, LANES), jnp.int32),
            pltpu.VMEM((depth, LANES), jnp.float32),
            pltpu.VMEM((n_col, chunk, LANES), jnp.float32),
            pltpu.VMEM((n_col, chunk, LANES), jnp.float32),
            pltpu.VMEM((n_row, chunk, LANES), jnp.float32),
            pltpu.VMEM((n_row, chunk, LANES), jnp.float32),
            dma((8,)),
            dma((n_col,)), dma((n_col,)), dma((n_row,)), dma((n_row,)),
            dma((n_col,)), dma((n_col,)), dma((n_row,)), dma((n_row,)),
        ],
        compiler_params=pltpu.CompilerParams(collective_id=0, has_side_effects=True),
        name="lanczos",
    )(x, w, tile_rows, tile_cols, tile_scale, tile_count, scale_table)
    return out.reshape(groups, NVEC, LANES).transpose(1, 0, 2).reshape(NVEC, piece_len)


def solution(mesh):
    return jax.shard_map(
        per_device,
        mesh=mesh,
        in_specs=(
            P(None, ("row", "col")),
            P("row", "col", None, None),
            P("row", "col", None),
            P("row", "col", None),
            P("row", "col", None),
            P("row", "col"),
            P(),
        ),
        out_specs=P(None, ("row", "col")),
        check_vma=False,
    )
```

time: 62.2 us -> 18.5 us (0.30)
  blocking collectives: 31.9 us -> 0 us
  Pallas kernels: 0 us -> 14 us
  between operations: 14.2 us -> 0.66 us
  other arithmetic: 4.82 us -> 0 us
  local copies, waits for them, and re-layouts: 7.3 us -> 3.56 us
  waiting for transfers between devices: 3.01 us -> 0 us
  matrix products: 0.74 us -> 0 us
    all_gather x2 -> x0, blocking collectives: 24.3 us -> none  [the longest x1 13.6 us: per_device(): lax.all_gather(vectors, 'col', axis=1, tiled=True)]
    pallas_call x0 -> x1, Pallas kernels: none -> 14 us  [per_device(): pl.pallas_call(functools.partial(kernel, n_row, n_col, slots, piece_len),...]
    all_to_all x1 -> x0, blocking collectives: 7.51 us -> none  [per_device(): lax.all_to_all(col_flat.reshape(NVEC, row_total, piece_len), 'row', split...]
    unnamed x14 -> x1, local copies, waits for them, and re-layouts: 5.06 us -> 1.3 us
    scatter-add x2 -> x0, other arithmetic: 3.3 us -> none  [the longest x1 1.65 us: tile_sums(): row_start.at[:, row_ids].add(forward)]
    unnamed x2 -> x0, waiting for transfers between devices: 3.01 us -> none
    reshape x4 -> x1, local copies, waits for them, and re-layouts: 0.29 us -> 2.26 us  [per_device(): w = tile_values.reshape(slots * TILE, TILE)]
    gather x2 -> x0, local copies, waits for them, and re-layouts: 1.23 us -> none  [the longest x1 0.61 us: tile_sums(): distant = jnp.take(col_vec, col_ids, axis=1)]
  transfers between devices with their start and end apart: 1 -> 0, of which waited for: 1 -> 0; matrix products, arithmetic and copies ran while one was open for 5% -> 0% of each run, Pallas kernels for 0% -> 0%
where the time goes in v1:
time: 18.5 us; the launch traced here: 18.2 us
  Pallas kernels  14 us (76%)
  local copies, waits for them, and re-layouts  3.56 us (19%)
  between operations  0.66 us (4%)
    pallas_call x1, Pallas kernels, per_device(): pl.pallas_call(functools.partial(kernel, n_row, n_col, slots, piece_len),...  14 us
    reshape x1, local copies, waits for them, and re-layouts, per_device(): w = tile_values.reshape(slots * TILE, TILE)  2.26 us
    unnamed x1, local copies, waits for them, and re-layouts  1.3 us

profile of v1, /device:TPU:0, one launch (start us, length us, event | category | flops | bytes accessed | tf_op | source)
XLA Modules:
  0.0 18.2 jit_solution(13019468719584776031)
XLA Ops:
  0.7 2.3 %reshape.17.w_hbm = bf16[2048,64]{1,0:T(8,128)(2,1)} reshape(bf16[1,1,32,4096]{3,2,1,0:T(8,128)(2,1)} %param.8) | data formatting | bytes 524288 | tf_op jit(solution)/shard_map/reshape | solution.py:202
  2.9 14.0 %lanczos.1 = f32[16,128]{1,0:T(8,128)} custom-call(bf16[16,128]{1,0:T(8,128)(2,1)} %bitcast.13, bf16[2048,64]{1,0:T(8,128)(2,1)} %reshape.17.w_hbm, s32[1,1,32]{2,1,0:T(1,128)} %rows_hbm.1, s32[1,1,32]{2,1,0:T(1,128)} %cols_hbm.1, s32[1,1,32]{2,1,0:T(1,128)} %scale_hbm.1, s32[1,1]{1,0:T(1,128)S(6)} %copy.13.count_hbm, f32[64]{0:T(128)} %table_hbm.1), custom_call_target="tpu_custom_call" | custom-call | tf_op jit(solution)/shard_map/lanczos/pallas_call | solution.py:204
  16.9 1.3 %copy.14 = f32[4,512]{1,0:T(4,128)} copy(f32[4,512]{1,0:T(4,128)} %bitcast.12) | data formatting | bytes 16384

commit v2 on v1

--- a/solution.py
+++ b/solution.py
@@ -14,11 +14,36 @@
 MESH = pl.DeviceIdType.MESH
 
 
+def relayout(slots, tv_vm, w32_vm, w_vm):
+    pack = LANES // TILE
+    step = max(1, 2 * LANES // (pack * slots))
+    depth = pack * step * slots
+    r = lax.broadcasted_iota(jnp.int32, (depth, depth), 0)
+    c = lax.broadcasted_iota(jnp.int32, (depth, depth), 1)
+    slot, i = lax.div(r, pack * step), lax.rem(r, pack * step)
+    source = (lax.rem(i, pack) * step + lax.div(i, pack)) * slots + slot
+    order = jnp.where(c == source, 1.0, 0.0).astype(jnp.bfloat16)
+    low_half = lax.broadcasted_iota(jnp.int32, (slots, LANES), 1) < TILE
+    total = TILE * TILE // LANES
+    for first in range(0, total, step):
+        low, high = [], []
+        for g in range(first, first + step):
+            part = tv_vm[:, g * LANES:(g + 1) * LANES].astype(jnp.float32)
+            turned = pltpu.roll(part, TILE, 1)
+            low.append(jnp.where(low_half, part, turned).astype(jnp.bfloat16))
+            high.append(jnp.where(low_half, turned, part).astype(jnp.bfloat16))
+        moved = jnp.dot(
+            order, jnp.concatenate(low + high, axis=0), preferred_element_type=jnp.float32)
+        w32_vm[:, first * pack:(first + step) * pack, :] = moved.reshape(
+            slots, pack * step, LANES)
+    w_vm[...] = w32_vm[...].reshape(slots * TILE, LANES).astype(jnp.bfloat16)
+
+
 def kernel(
     n_row, n_col, slots, piece_len,
     x_hbm, w_hbm, rows_hbm, cols_hbm, scale_hbm, count_hbm, table_hbm,
     out_ref,
-    col_x, row_x, w_vm, rows_sm, cols_sm, scale_sm, count_sm, table_sm,
+    col_x, row_x, tv_vm, w32_vm, w_vm, rows_sm, cols_sm, scale_sm, count_sm, table_sm,
     rid_vm, cid_vm, wt_vm, row_send, row_recv, col_send, col_recv,
     local_sem, x_row_send, x_row_recv, x_col_send, x_col_recv,
     p_row_send, p_row_recv, p_col_send, p_col_recv,
@@ -39,7 +64,7 @@
             (scale_hbm, scale_sm),
             (count_hbm, count_sm),
             (table_hbm, table_sm),
-            (w_hbm, w_vm),
+            (w_hbm, tv_vm),
         ))
     ]
     for copy in copies:
@@ -75,6 +100,8 @@
     for copy in gather_row + gather_col:
         copy.start()
 
+    copies[7].wait()
+    relayout(slots, tv_vm, w32_vm, w_vm)
     for copy in copies[2:7]:
         copy.wait()
     upper = lax.broadcasted_iota(jnp.int32, (8, LANES), 0) < NVEC
@@ -127,7 +154,6 @@
     g_row = lax.div(lax.broadcasted_iota(jnp.int32, (rows_of, wide), 0), NVEC)
     g_col = lax.div(lax.broadcasted_iota(jnp.int32, (rows_of, wide), 1), TILE)
     same = g_row == g_col
-    copies[7].wait()
 
     for copy in gather_col:
         copy.wait_recv()
@@ -136,7 +162,8 @@
     for g in range(slots // GROUP):
         tiles = w_vm[g * wide:(g + 1) * wide, :]
         prod = lax.dot_general(
-            distant[g * rows_of:(g + 1) * rows_of, :TILE], tiles, (((1,), (1,)), ((), ())),
+            distant[g * rows_of:(g + 1) * rows_of, :TILE], tiles[:, :TILE],
+            (((1,), (1,)), ((), ())),
             preferred_element_type=jnp.float32)
         prod = jnp.where(same, prod, 0.0)
         total = prod[:, :LANES]
@@ -163,8 +190,7 @@
         left = near[g * rows_of:(g + 1) * rows_of, :]
         left = jnp.concatenate([left] * (wide // LANES), axis=1)
         left = jnp.where(same, left, jnp.zeros_like(left))
-        prod = jnp.dot(left, tiles, preferred_element_type=jnp.float32)
-        parts.append(jnp.concatenate([prod, prod], axis=1))
+        parts.append(jnp.dot(left, tiles, preferred_element_type=jnp.float32))
     mirrored = jnp.concatenate(parts, axis=0) * col_weight
     col_send[...] = place(put_col, mirrored).reshape(n_row, chunk, LANES)
     scatter_col = [
@@ -199,17 +225,19 @@
     chunk = groups * NVEC
     depth = slots * NVEC
     x = vectors.reshape(NVEC, groups, LANES).transpose(1, 0, 2).reshape(chunk, LANES)
-    w = tile_values.reshape(slots * TILE, TILE)
+    w = tile_values.reshape(slots, TILE * TILE)
     dma = pltpu.SemaphoreType.DMA
     out = pl.pallas_call(
         functools.partial(kernel, n_row, n_col, slots, piece_len),
         out_shape=jax.ShapeDtypeStruct((chunk, LANES), jnp.float32),
-        in_specs=[pl.BlockSpec(memory_space=pl.ANY)] * 7,
+        in_specs=[pl.BlockSpec(memory_space=pltpu.HBM)] * 7,
         out_specs=pl.BlockSpec(memory_space=pltpu.VMEM),
         scratch_shapes=[
             pltpu.VMEM((n_row, chunk, LANES), jnp.bfloat16),
             pltpu.VMEM((n_col, chunk, LANES), jnp.bfloat16),
-            pltpu.VMEM((slots * TILE, TILE), jnp.bfloat16),
+            pltpu.VMEM((slots, TILE * TILE), jnp.bfloat16),
+            pltpu.VMEM((slots, TILE, LANES), jnp.float32),
+            pltpu.VMEM((slots * TILE, LANES), jnp.bfloat16),
             pltpu.SMEM(tile_rows.shape, jnp.int32),
             pltpu.SMEM(tile_cols.shape, jnp.int32),
             pltpu.SMEM(tile_scale.shape, jnp.int32),
@@ -226,7 +254,7 @@
             dma((n_col,)), dma((n_col,)), dma((n_row,)), dma((n_row,)),
             dma((n_col,)), dma((n_col,)), dma((n_row,)), dma((n_row,)),
         ],
-        compiler_params=pltpu.CompilerParams(collective_id=0, has_side_effects=True),
+        compiler_params=pltpu.CompilerParams(collective_id=0, has_side_effects=True, vmem_limit_bytes=24 * 1024 * 1024),
         name="lanczos",
     )(x, w, tile_rows, tile_cols, tile_scale, tile_count, scale_table)
     return out.reshape(groups, NVEC, LANES).transpose(1, 0, 2).reshape(NVEC, piece_len)

time: 18.5 us -> 17.1 us (0.924)
  local copies, waits for them, and re-layouts: 3.56 us -> 2.86 us
  Pallas kernels: 14 us -> 13.4 us
    reshape x1 -> x0, local copies, waits for them, and re-layouts: 2.26 us -> none  [per_device(): w = tile_values.reshape(slots * TILE, TILE)]
    unnamed x1 -> x13, local copies, waits for them, and re-layouts: 1.3 us -> 2.86 us
    pallas_call x1, Pallas kernels: 14 us -> 13.4 us  [per_device(): pl.pallas_call(functools.partial(kernel, n_row, n_col, slots, piece_len),...]
where the time goes in v2:
time: 17.1 us; the launch traced here: 16.9 us
  Pallas kernels  13.4 us (78%)
  local copies, waits for them, and re-layouts  2.86 us (17%)
  between operations  0.71 us (4%)
    pallas_call x1, Pallas kernels, per_device(): pl.pallas_call(functools.partial(kernel, n_row, n_col, slots, piece_len),...  13.4 us
    unnamed x13, local copies, waits for them, and re-layouts  2.86 us

profile of v2, /device:TPU:0, one launch (start us, length us, event | category | flops | bytes accessed | tf_op | source)
XLA Modules:
  0.0 16.9 jit_solution(4572035488497536901)
XLA Ops:
  0.0 0.0 copy-start.1
  0.7 0.0 copy-start.2
  0.7 0.0 copy-start.3
  0.7 0.0 copy-start.4
  0.7 0.0 copy-done.1
  0.7 0.6 %copy-done.2 = s32[1,1,32]{2,1,0:T(1,128)S(1)} copy-done((s32[1,1,32]{2,1,0:T(1,128)S(1)}, s32[1,1,32]{2,1,0:T(1,128)}, u32[]{:S(2)}) %copy-start.2) | copy-done | bytes 152
  1.3 0.0 copy-done.3
  1.3 0.0 copy-done.4
  1.4 0.0 copy-start
  1.4 0.9 %copy-done = bf16[1,1,32,4096]{3,2,1,0:T(8,128)(2,1)S(1)} copy-done((bf16[1,1,32,4096]{3,2,1,0:T(8,128)(2,1)S(1)}, bf16[1,1,32,4096]{3,2,1,0:T(8,128)(2,1)}, u32[]{:S(2)}) %copy-start) | copy-done | bytes 262168
  2.3 0.0 copy-start.5
  2.3 0.7 %copy-done.5 = f32[64]{0:T(128)S(1)} copy-done((f32[64]{0:T(128)S(1)}, f32[64]{0:T(128)}, u32[]{:S(2)}) %copy-start.5) | copy-done | bytes 280
  3.0 13.4 %lanczos.1 = f32[16,128]{1,0:T(8,128)S(1)} custom-call(bf16[16,128]{1,0:T(8,128)(2,1)S(1)} %bitcast.13, bf16[32,4096]{1,0:T(8,128)(2,1)S(1)} %bitcast.11, s32[1,1,32]{2,1,0:T(1,128)S(1)} %copy-done.2, s32[1,1,32]{2,1,0:T(1,128)S(1)} %copy-done.3, s32[1,1,32]{2,1,0:T(1,128)S(1)} %copy-done.4, s32[1,1]{1,0:T(1,128)S(6)} %copy.11.count_hbm, f32[64]{0:T(128)S(1)} %copy-done.5), custom_call_target="tpu_custom_call" | custom-call | tf_op jit(solution)/shard_map/lanczos/pallas_call | solution.py:230
  16.3 0.6 %copy.12 = f32[4,512]{1,0:T(4,128)} copy(f32[4,512]{1,0:T(4,128)S(1)} %bitcast.12) | data formatting | bytes 16384
Async XLA Ops:
  0.0 0.7 %copy-start.1 = (bf16[4,512]{1,0:T(4,128)(2,1)S(1)}, bf16[4,512]{1,0:T(4,128)(2,1)}, u32[]{:S(2)}) copy-start(bf16[4,512]{1,0:T(4,128)(2,1)} %param.7) | copy-start | bytes 12292
  0.7 0.7 %copy-start.2 = (s32[1,1,32]{2,1,0:T(1,128)S(1)}, s32[1,1,32]{2,1,0:T(1,128)}, u32[]{:S(2)}) copy-start(s32[1,1,32]{2,1,0:T(1,128)} %rows_hbm.1) | copy-start | bytes 388
  0.7 0.7 %copy-start.3 = (s32[1,1,32]{2,1,0:T(1,128)S(1)}, s32[1,1,32]{2,1,0:T(1,128)}, u32[]{:S(2)}) copy-start(s32[1,1,32]{2,1,0:T(1,128)} %cols_hbm.1) | copy-start | bytes 388
  0.7 0.7 %copy-start.4 = (s32[1,1,32]{2,1,0:T(1,128)S(1)}, s32[1,1,32]{2,1,0:T(1,128)}, u32[]{:S(2)}) copy-start(s32[1,1,32]{2,1,0:T(1,128)} %scale_hbm.1) | copy-start | bytes 388
  1.4 0.9 %copy-start = (bf16[1,1,32,4096]{3,2,1,0:T(8,128)(2,1)S(1)}, bf16[1,1,32,4096]{3,2,1,0:T(8,128)(2,1)}, u32[]{:S(2)}) copy-start(bf16[1,1,32,4096]{3,2,1,0:T(8,128)(2,1)} %param.8) | copy-start | bytes 786436
  2.3 0.7 %copy-start.5 = (f32[64]{0:T(128)S(1)}, f32[64]{0:T(128)}, u32[]{:S(2)}) copy-start(f32[64]{0:T(128)} %table_hbm.1) | copy-start | bytes 772

commit v3 on v2

--- a/solution.py
+++ b/solution.py
@@ -229,7 +229,7 @@
     dma = pltpu.SemaphoreType.DMA
     out = pl.pallas_call(
         functools.partial(kernel, n_row, n_col, slots, piece_len),
-        out_shape=jax.ShapeDtypeStruct((chunk, LANES), jnp.float32),
+        out_shape=pltpu.VMEM((chunk, LANES), jnp.float32),
         in_specs=[pl.BlockSpec(memory_space=pltpu.HBM)] * 7,
         out_specs=pl.BlockSpec(memory_space=pltpu.VMEM),
         scratch_shapes=[
@@ -254,7 +254,7 @@
             dma((n_col,)), dma((n_col,)), dma((n_row,)), dma((n_row,)),
             dma((n_col,)), dma((n_col,)), dma((n_row,)), dma((n_row,)),
         ],
-        compiler_params=pltpu.CompilerParams(collective_id=0, has_side_effects=True, vmem_limit_bytes=24 * 1024 * 1024),
+        compiler_params=pltpu.CompilerParams(collective_id=0, has_side_effects=True),
         name="lanczos",
     )(x, w, tile_rows, tile_cols, tile_scale, tile_count, scale_table)
     return out.reshape(groups, NVEC, LANES).transpose(1, 0, 2).reshape(NVEC, piece_len)

time: 17.1 us -> 14.8 us (0.87)
  local copies, waits for them, and re-layouts: 2.86 us -> 0.6 us
    unnamed x13 -> x1, local copies, waits for them, and re-layouts: 2.86 us -> 0.6 us
where the time goes in v3:
time: 14.8 us; the launch traced here: 14.6 us
  Pallas kernels  13.4 us (91%)
  between operations  0.66 us (4%)
  local copies, waits for them, and re-layouts  0.6 us (4%)
    pallas_call x1, Pallas kernels, per_device(): pl.pallas_call(functools.partial(kernel, n_row, n_col, slots, piece_len),...  13.4 us
    unnamed x1, local copies, waits for them, and re-layouts  0.6 us

profile of v3, /device:TPU:0, one launch (start us, length us, event | category | flops | bytes accessed | tf_op | source)
XLA Modules:
  0.0 14.6 jit_solution(12543822970396079820)
XLA Ops:
  0.7 13.4 %lanczos.1 = f32[16,128]{1,0:T(8,128)S(1)} custom-call(bf16[16,128]{1,0:T(8,128)(2,1)} %bitcast.13, bf16[32,4096]{1,0:T(8,128)(2,1)} %bitcast.12, s32[1,1,32]{2,1,0:T(1,128)} %rows_hbm.1, s32[1,1,32]{2,1,0:T(1,128)} %cols_hbm.1, s32[1,1,32]{2,1,0:T(1,128)} %scale_hbm.1, s32[1,1]{1,0:T(1,128)S(6)} %copy.12.count_hbm, f32[64]{0:T(128)} %table_hbm.1), custom_call_target="tpu_custom_call" | custom-call | tf_op jit(solution)/shard_map/lanczos/pallas_call | solution.py:230
  14.0 0.6 %copy.11 = f32[4,512]{1,0:T(4,128)} copy(f32[4,512]{1,0:T(4,128)S(1)} %bitcast.11) | data formatting | bytes 16384
